TPU v7x, 32 devices: a whole 2x2x4 slice. The times are simulated.
32 devices in a mesh: groups: 2 (over x), tensor: 4 (over y, core), section: 4 (over z).
Axes of the slice: x: 2, y: 2, z: 4, core: 2. Of those that a mesh axis runs over, the one named last changes fastest.
Arguments:
- prompt: bfloat16 [128, 8192], P(('groups', 'section'), 'tensor'), parts along dimension 0, may hold values from -6 to 6
- norm_gain: float32 [8, 8192], P(('groups', 'section')), parts along dimension 0, may hold values from 0.5 to 1.5
- kept_ranks: int32 [8, 3], P(('groups', 'section')), parts along dimension 0, may hold values from 128 to 512, as said below
- gate_left: bfloat16 [8, 512, 8192], P('groups', 'tensor', 'section'), parts along dimension 0, may hold values from -0.0625 to 0.0625
- up_left: bfloat16 [8, 512, 8192], P('groups', 'tensor', 'section'), parts along dimension 0, may hold values from -0.0625 to 0.0625
- gate_right: bfloat16 [8, 512, 14336], P('groups', 'tensor', 'section'), parts along dimension 0, may hold values from -0.375 to 0.375
- up_right: bfloat16 [8, 512, 14336], P('groups', 'tensor', 'section'), parts along dimension 0, may hold values from -0.375 to 0.375
- down_left: bfloat16 [8, 512, 14336], P('groups', 'tensor', 'section'), parts along dimension 0, may hold values from -0.046875 to 0.046875
- down_right: bfloat16 [8, 8192, 512], P('groups', 'tensor', 'section'), parts along dimension 0, may hold values from -0.5 to 0.5
Outputs:
- final_stream: bfloat16 [128, 8192], P(('groups', 'section'), 'tensor'), parts along dimension 0
There are 2 independent parts, one for each index of `groups`. A program takes and returns all parts, laid end to end along the dimension named above; each array names one. Nothing has to cross between parts.
Inputs may be any that keep to these rules, and one draw needn't show every extreme that they name: `kept_ranks`: column 0, 1, 2 holds the rank kept for the gate, up and down matrices; the value 512 occurs in every draw.
All inputs are finite; a program needn't handle non-finite values.
Results may differ from a plain program's by a relative error of at most 0.035.
Values may be sent and summed in bfloat16 or wider, within the bound.
No kernel may reach another device: no remote copies, remote signals or barrier semaphores. Data moves between devices by JAX's collectives and lax.ppermute only.
A program may use at most 128 MiB of HBM per device.

v0:
```python
import jax
import jax.numpy as jnp
from jax import lax
from jax.sharding import PartitionSpec as P

RMAX = 512


def from_behind(block, axis, distance):
    devices = range(lax.axis_size(axis))
    route = [(i - distance, i) for i in devices if i - distance in devices]
    return lax.ppermute(block, axis, route)


def broadcast(array, axis, root):
    mine = lax.axis_index(axis) == root
    return lax.psum(jnp.where(mine, array, jnp.zeros_like(array)), axis)


def contract_last(left_side, right_side):
    return lax.dot_general(
        left_side, right_side, (((1,), (1,)), ((), ())), preferred_element_type=jnp.float32
    )


def body(
    prompt, norm_gain, kept_ranks, gate_left, up_left, gate_right, up_right, down_left, down_right
):
    section_count = lax.axis_size("section")
    tensor_rank = lax.axis_index("tensor")
    section_rank = lax.axis_index("section")
    gate_rows, up_rows, down_cols = (
        lax.all_to_all(gate_left, "section", split_axis=0, concat_axis=2, tiled=True),
        lax.all_to_all(up_left, "section", split_axis=0, concat_axis=2, tiled=True),
        lax.all_to_all(down_right, "section", split_axis=0, concat_axis=2, tiled=True),
    )
    gate_cols, up_cols, down_rows = (
        lax.all_to_all(
            lax.all_to_all(gate_right, "tensor", split_axis=2, concat_axis=1, tiled=True),
            "section",
            split_axis=0,
            concat_axis=2,
            tiled=True,
        ),
        lax.all_to_all(
            lax.all_to_all(up_right, "tensor", split_axis=2, concat_axis=1, tiled=True),
            "section",
            split_axis=0,
            concat_axis=2,
            tiled=True,
        ),
        lax.all_to_all(
            lax.all_to_all(down_left, "tensor", split_axis=2, concat_axis=1, tiled=True),
            "section",
            split_axis=0,
            concat_axis=2,
            tiled=True,
        ),
    )
    gate_rows, up_rows, down_cols = (gate_rows[0], up_rows[0], down_cols[0])
    gate_cols, up_cols, down_rows = (gate_cols[0], up_cols[0], down_rows[0])
    rank_block = gate_rows.shape[0]
    column_block = down_cols.shape[0]
    micro_rows = prompt.shape[0]
    positions = tensor_rank * rank_block + jnp.arange(rank_block, dtype=jnp.int32)
    gate_mask = (positions < kept_ranks[0, 0]).astype(jnp.float32)
    up_mask = (positions < kept_ranks[0, 1]).astype(jnp.float32)
    down_mask = (jnp.arange(RMAX, dtype=jnp.int32) < kept_ranks[0, 2]).astype(jnp.float32)
    norm_scale = norm_gain[0]
    own_start = tensor_rank * column_block
    prompt_rows = lax.all_gather(prompt, "section", axis=0, tiled=True)

    def layer_step(stream):
        float_stream = stream.astype(jnp.float32)
        variance = jnp.mean(float_stream * float_stream, axis=-1, keepdims=True)
        normed = (float_stream * lax.rsqrt(variance + 1e-05) * norm_scale).astype(jnp.bfloat16)
        gate_part = (contract_last(normed, gate_rows) * gate_mask).astype(jnp.bfloat16)
        up_part = (contract_last(normed, up_rows) * up_mask).astype(jnp.bfloat16)
        gate_low, up_low = (
            lax.all_gather(gate_part, "tensor", axis=1, tiled=True),
            lax.all_gather(up_part, "tensor", axis=1, tiled=True),
        )
        gate_values = jnp.dot(gate_low, gate_cols, preferred_element_type=jnp.float32)
        up_values = jnp.dot(up_low, up_cols, preferred_element_type=jnp.float32)
        hidden = (jax.nn.silu(gate_values) * up_values).astype(jnp.bfloat16)
        summed = lax.psum(contract_last(hidden, down_rows), "tensor")
        down_low = (summed * down_mask).astype(jnp.bfloat16)
        branch = contract_last(down_low, down_cols)
        own_columns = lax.dynamic_slice_in_dim(float_stream, own_start, column_block, 1)
        return (own_columns + branch).astype(jnp.bfloat16)

    incoming = jnp.zeros((micro_rows, column_block), jnp.bfloat16)
    results = jnp.zeros((micro_rows * section_count, column_block), jnp.bfloat16)

    def tick_body(tick_index, carry):
        incoming, results = carry
        entering = lax.dynamic_slice_in_dim(
            prompt_rows, jnp.minimum(tick_index, section_count - 1) * micro_rows, micro_rows, 0
        )
        current = jnp.where((section_rank == 0) & (tick_index < section_count), entering, incoming)
        stream = lax.all_gather(current, "tensor", axis=1, tiled=True)
        new_part = layer_step(stream)
        incoming = from_behind(new_part, "section", 1)
        finished = tick_index - (section_count - 1)
        slot_start = jnp.maximum(finished, 0) * micro_rows
        updated = lax.dynamic_update_slice_in_dim(results, new_part, slot_start, 0)
        results = jnp.where((section_rank == section_count - 1) & (finished >= 0), updated, results)
        return (incoming, results)

    incoming, results = lax.fori_loop(0, 2 * section_count - 1, tick_body, (incoming, results))
    delivered = broadcast(results, "section", section_count - 1)
    return lax.dynamic_slice_in_dim(delivered, section_rank * micro_rows, micro_rows, 0)


def solution(mesh):
    in_specs = (
        P(("groups", "section"), "tensor"),
        P(("groups", "section"), None),
        P(("groups", "section"), None),
        P("groups", "tensor", "section"),
        P("groups", "tensor", "section"),
        P("groups", "tensor", "section"),
        P("groups", "tensor", "section"),
        P("groups", "tensor", "section"),
        P("groups", "tensor", "section"),
    )
    out_specs = P(("groups", "section"), "tensor")
    return jax.shard_map(body, mesh=mesh, in_specs=in_specs, out_specs=out_specs, check_vma=False)
```

profile of v0, /device:TPU:0, one launch (start us, length us, event | category | flops | bytes accessed | tf_op | source)
XLA Modules:
  0.0 1003.2 jit_solution(816205238414276463)
XLA Ops:
  6.5 6.8 copy.26
  18.2 6.9 copy.30
  25.0 36.4 %all-to-all-done.1 = bf16[4,128,3584]{1,0,2:T(4,128)(2,1)} async-done(((bf16[4,128,3584]{1,0,2:T(4,128)(2,1)}), bf16[4,128,3584]{1,0,2:T(4,128)(2,1)}, u32[]{:S(2)}, u32[]{:S(2)}) %all-to-all-start.1) | async-done | bytes 3670048 | tf_op jit(solution)/shard_map/all_to_all | solution.py:39
  66.2 6.9 copy.33
  73.0 35.7 %all-to-all-done.4 = bf16[4,128,3584]{1,0,2:T(4,128)(2,1)} async-done(((bf16[4,128,3584]{1,0,2:T(4,128)(2,1)}), bf16[4,128,3584]{1,0,2:T(4,128)(2,1)}, u32[]{:S(2)}, u32[]{:S(2)}) %all-to-all-start.4) | async-done | bytes 3670048 | tf_op jit(solution)/shard_map/all_to_all | solution.py:46
  108.7 48.1 %all_to_all.144 = bf16[4,128,3584]{1,0,2:T(4,128)(2,1)} all-to-all(bf16[4,128,3584]{1,0,2:T(4,128)(2,1)} %copy.33), channel_id=1, replica_groups=mesh['groups'=2,'tensor'=4,'section'=4] {'tensor'}, dimensions={2} | all-to-all | bytes 7340032 | tf_op jit(solution)/shard_map/all_to_all | solution.py:53
  156.8 53.6 %all_to_all.145 = bf16[4,128,2048]{2,1,0:T(8,128)(2,1)} all-to-all(bf16[4,128,2048]{2,1,0:T(8,128)(2,1)S(1)} %copy-done.6), channel_id=1, replica_groups=mesh['groups'=2,'tensor'=4,'section'=4] {'section'}, dimensions={0} | all-to-all | bytes 4194304 | tf_op jit(solution)/shard_map/all_to_all | solution.py:33
  210.4 50.4 %all_to_all.146 = bf16[4,128,2048]{2,1,0:T(8,128)(2,1)} all-to-all(bf16[4,128,2048]{2,1,0:T(8,128)(2,1)S(1)} %copy-done.7), channel_id=1, replica_groups=mesh['groups'=2,'tensor'=4,'section'=4] {'section'}, dimensions={0} | all-to-all | bytes 4194304 | tf_op jit(solution)/shard_map/all_to_all | solution.py:34
  264.5 6.9 copy.27
  271.3 40.4 %all-to-all-done.8 = bf16[4,2048,128]{2,1,0:T(8,128)(2,1)S(1)} async-done(((bf16[4,2048,128]{2,1,0:T(8,128)(2,1)}), bf16[4,2048,128]{2,1,0:T(8,128)(2,1)S(1)}, u32[]{:S(2)}, u32[]{:S(2)}) %all-to-all-start.8) | async-done | bytes 2097184 | tf_op jit(solution)/shard_map/all_to_all | solution.py:35
  317.8 6.9 copy.31
  324.7 74.6 %all-to-all-done.2 = bf16[4,512,896]{2,1,0:T(8,128)(2,1)} async-done(((bf16[4,512,896]{2,1,0:T(8,128)(2,1)}), bf16[4,512,896]{2,1,0:T(8,128)(2,1)}, u32[]{:S(2)}, u32[]{:S(2)}) %all-to-all-start.2) | async-done | bytes 3670048 | tf_op jit(solution)/shard_map/all_to_all | solution.py:38
  404.1 7.0 copy.34
  411.0 74.6 %all-to-all-done.5 = bf16[4,512,896]{2,1,0:T(8,128)(2,1)} async-done(((bf16[4,512,896]{2,1,0:T(8,128)(2,1)}), bf16[4,512,896]{2,1,0:T(8,128)(2,1)}, u32[]{:S(2)}, u32[]{:S(2)}) %all-to-all-start.5) | async-done | bytes 3670048 | tf_op jit(solution)/shard_map/all_to_all | solution.py:45
  490.6 89.0 %all_gather.33 = bf16[64,2048]{1,0:T(8,128)(2,1)S(1)} all-gather(bf16[16,2048]{1,0:T(8,128)(2,1)S(1)} %copy-done.8), channel_id=1, replica_groups=mesh['groups'=2,'tensor'=4,'section'=4] {'section'}, dimensions={0}, use_global_device_ids=true | all-gather | bytes 327680 | tf_op jit(solution)/shard_map/all_gather | solution.py:71
  587.6 9.7 copy.36
  599.1 6.0 copy.28
  605.0 5.9 copy.37
  611.0 6.0 copy.32
  616.9 6.0 copy.38
  622.9 6.0 copy.35
  628.9 6.0 copy.39
  634.9 322.3 %while.19 = (s32[]{:T(128)}, bf16[16,2048]{1,0:T(8,128)(2,1)S(1)}, bf16[64,2048]{1,0:T(8,128)(2,1)S(1)}, pred[]{:T(512)}, bf16[64,2048]{1,0:T(8,128)(2,1)S(1)}, ...) while((s32[]{:T(128)}, bf16[16,2048]{1,0:T(8,128)(2,1)S(1)}, ...), condition=%wide.region_3.4_spmd.clone.clone, body=%wide.region_0.3_spmd.clone.clone.sunk | while | flops 278906656 | bytes 35412760 | solution.py:110
  635.0 5.8 all_gather.43
  642.5 5.2 all_gather.45
  650.6 5.2 all_gather.44
  661.0 11.4 %psum.25 = f32[16,512]{1,0:T(8,128)S(1)} all-reduce(f32[16,512]{1,0:T(8,128)S(1)} %fusion.54), channel_id=1, replica_groups=mesh['groups'=2,'tensor'=4,'section'=4] {'tensor'}, use_global_device_ids=true, to_apply=%region_2.2 | all-reduce | flops 8192 | bytes 65536 | tf_op jit(solution)/shard_map/while/body/eval_jaxpr/psum | solution.py:86
  680.1 5.8 all_gather.43
  687.6 5.2 all_gather.45
  695.7 5.2 all_gather.44
  706.1 10.9 %psum.25 = f32[16,512]{1,0:T(8,128)S(1)} all-reduce(f32[16,512]{1,0:T(8,128)S(1)} %fusion.54), channel_id=1, replica_groups=mesh['groups'=2,'tensor'=4,'section'=4] {'tensor'}, use_global_device_ids=true, to_apply=%region_2.2 | all-reduce | flops 8192 | bytes 65536 | tf_op jit(solution)/shard_map/while/body/eval_jaxpr/psum | solution.py:86
  726.0 5.8 all_gather.43
  733.5 5.2 all_gather.45
  741.6 5.2 all_gather.44
  752.1 11.4 %psum.25 = f32[16,512]{1,0:T(8,128)S(1)} all-reduce(f32[16,512]{1,0:T(8,128)S(1)} %fusion.54), channel_id=1, replica_groups=mesh['groups'=2,'tensor'=4,'section'=4] {'tensor'}, use_global_device_ids=true, to_apply=%region_2.2 | all-reduce | flops 8192 | bytes 65536 | tf_op jit(solution)/shard_map/while/body/eval_jaxpr/psum | solution.py:86
  772.5 5.8 all_gather.43
  788.1 5.2 all_gather.44
  798.5 10.9 %psum.25 = f32[16,512]{1,0:T(8,128)S(1)} all-reduce(f32[16,512]{1,0:T(8,128)S(1)} %fusion.54), channel_id=1, replica_groups=mesh['groups'=2,'tensor'=4,'section'=4] {'tensor'}, use_global_device_ids=true, to_apply=%region_2.2 | all-reduce | flops 8192 | bytes 65536 | tf_op jit(solution)/shard_map/while/body/eval_jaxpr/psum | solution.py:86
  818.4 5.8 all_gather.43
  825.9 5.2 all_gather.45
  844.5 11.4 %psum.25 = f32[16,512]{1,0:T(8,128)S(1)} all-reduce(f32[16,512]{1,0:T(8,128)S(1)} %fusion.54), channel_id=1, replica_groups=mesh['groups'=2,'tensor'=4,'section'=4] {'tensor'}, use_global_device_ids=true, to_apply=%region_2.2 | all-reduce | flops 8192 | bytes 65536 | tf_op jit(solution)/shard_map/while/body/eval_jaxpr/psum | solution.py:86
  864.9 5.8 all_gather.43
  880.5 5.2 all_gather.44
  890.9 10.9 %psum.25 = f32[16,512]{1,0:T(8,128)S(1)} all-reduce(f32[16,512]{1,0:T(8,128)S(1)} %fusion.54), channel_id=1, replica_groups=mesh['groups'=2,'tensor'=4,'section'=4] {'tensor'}, use_global_device_ids=true, to_apply=%region_2.2 | all-reduce | flops 8192 | bytes 65536 | tf_op jit(solution)/shard_map/while/body/eval_jaxpr/psum | solution.py:86
  910.8 5.8 all_gather.43
  918.3 5.2 all_gather.45
  936.9 11.4 %psum.25 = f32[16,512]{1,0:T(8,128)S(1)} all-reduce(f32[16,512]{1,0:T(8,128)S(1)} %fusion.54), channel_id=1, replica_groups=mesh['groups'=2,'tensor'=4,'section'=4] {'tensor'}, use_global_device_ids=true, to_apply=%region_2.2 | all-reduce | flops 8192 | bytes 65536 | tf_op jit(solution)/shard_map/while/body/eval_jaxpr/psum | solution.py:86
  958.0 36.9 %all-reduce.2.cloned.1.call-done = bf16[64,2048]{1,0:T(8,128)(2,1)} async-done(((bf16[64,2048]{1,0:T(8,128)(2,1)}), bf16[64,2048]{1,0:T(8,128)(2,1)}) %all-reduce.2.cloned.1.call-update) | async-done | bytes 262160 | tf_op jit(solution)/shard_map/psum | solution.py:17
  (153 shorter events, 192.2 us)
Async XLA Ops:
  13.4 48.0 %all-to-all-start.1 = ((bf16[4,128,3584]{1,0,2:T(4,128)(2,1)}), bf16[4,128,3584]{1,0,2:T(4,128)(2,1)}, u32[]{:S(2)}, u32[]{:S(2)}) async-start(bf16[4,128,3584]{1,0,2:T(4,128)(2,1)} %copy.26), calls=%async_computation.1 | async-start | bytes 7340032 | tf_op jit(solution)/shard_map/all_to_all | solution.py:39
  61.4 47.3 %all-to-all-start.4 = ((bf16[4,128,3584]{1,0,2:T(4,128)(2,1)}), bf16[4,128,3584]{1,0,2:T(4,128)(2,1)}, u32[]{:S(2)}, u32[]{:S(2)}) async-start(bf16[4,128,3584]{1,0,2:T(4,128)(2,1)} %copy.30), calls=%async_computation.4 | async-start | bytes 7340032 | tf_op jit(solution)/shard_map/all_to_all | solution.py:46
  73.0 83.8 %copy-start.6 = (bf16[4,128,2048]{2,1,0:T(8,128)(2,1)S(1)}, bf16[4,128,2048]{2,1,0:T(8,128)(2,1)}, u32[]{:S(2)}) copy-start(bf16[4,128,2048]{2,1,0:T(8,128)(2,1)} %param.14) | copy-start | bytes 6291460
  156.8 53.6 %copy-start.7 = (bf16[4,128,2048]{2,1,0:T(8,128)(2,1)S(1)}, bf16[4,128,2048]{2,1,0:T(8,128)(2,1)}, u32[]{:S(2)}) copy-start(bf16[4,128,2048]{2,1,0:T(8,128)(2,1)} %param.15) | copy-start | bytes 6291460
  260.8 50.9 %all-to-all-start.8 = ((bf16[4,2048,128]{2,1,0:T(8,128)(2,1)}), bf16[4,2048,128]{2,1,0:T(8,128)(2,1)S(1)}, u32[]{:S(2)}, u32[]{:S(2)}) async-start(bf16[4,2048,128]{2,1,0:T(8,128)(2,1)} %param.19), calls=%async_computation.8 | async-start | bytes 4194304 | tf_op jit(solution)/shard_map/all_to_all | solution.py:35
  311.7 1.3 copy-start.1
  313.0 86.3 %all-to-all-start.2 = ((bf16[4,512,896]{2,1,0:T(8,128)(2,1)}), bf16[4,512,896]{2,1,0:T(8,128)(2,1)}, u32[]{:S(2)}, u32[]{:S(2)}) async-start(bf16[4,512,896]{2,1,0:T(8,128)(2,1)} %bitcast.83), calls=%async_computation.2 | async-start | bytes 7340032 | tf_op jit(solution)/shard_map/all_to_all | solution.py:38
  399.3 86.3 %all-to-all-start.5 = ((bf16[4,512,896]{2,1,0:T(8,128)(2,1)}), bf16[4,512,896]{2,1,0:T(8,128)(2,1)}, u32[]{:S(2)}, u32[]{:S(2)}) async-start(bf16[4,512,896]{2,1,0:T(8,128)(2,1)} %bitcast.82), calls=%async_computation.5 | async-start | bytes 7340032 | tf_op jit(solution)/shard_map/all_to_all | solution.py:45
  485.6 5.0 copy-start.8
  485.6 94.0 %copy-start.9 = (s32[1,3]{1,0:T(1,128)S(1)}, s32[1,3]{1,0:T(1,128)}, u32[]{:S(2)}) copy-start(s32[1,3]{1,0:T(1,128)} %param.13) | copy-start | bytes 40
  485.6 94.6 %copy-start.4 = (bf16[4,128,2048]{2,1,0:T(8,128)(2,1)S(1)}, bf16[4,128,2048]{2,1,0:T(8,128)(2,1)}, u32[]{:S(2)}) copy-start(bf16[4,128,2048]{2,1,0:T(8,128)(2,1)} %all_to_all.145) | copy-start | bytes 6291460
  485.6 137.3 %all-to-all-start.7 = ((bf16[4,512,896]{2,1,0:T(8,128)(2,1)}), bf16[4,512,896]{2,1,0:T(8,128)(2,1)}, u32[]{:S(2)}, u32[]{:S(2)}) async-start(bf16[4,512,896]{2,1,0:T(8,128)(2,1)} %bitcast.80), calls=%async_computation.7 | async-start | bytes 7340032 | tf_op jit(solution)/shard_map/all_to_all | solution.py:52
  490.5 504.4 %all-reduce.2.cloned.1.call-start = ((), (), s32[]{:S(2)}) async-start(), calls=%async_computation.9 | async-start | bytes 524288 | tf_op jit(solution)/shard_map/psum | solution.py:17
  580.2 3.1 copy-start.3
  583.3 4.4 copy-start.2
  628.9 6.0 copy-start.5
  641.0 14.8 %copy-start = (bf16[512,3584]{1,0:T(8,128)(2,1)S(1)}, bf16[512,3584]{1,0:T(8,128)(2,1)}, u32[]{:S(2)}) copy-start(bf16[512,3584]{1,0:T(8,128)(2,1)} %get-tuple-element.710) | copy-start | bytes 11010052 | tf_op jit(solution)/shard_map/while
  675.3 4.8 collective-permute-start
  686.1 14.8 %copy-start = (bf16[512,3584]{1,0:T(8,128)(2,1)S(1)}, bf16[512,3584]{1,0:T(8,128)(2,1)}, u32[]{:S(2)}) copy-start(bf16[512,3584]{1,0:T(8,128)(2,1)} %get-tuple-element.710) | copy-start | bytes 11010052 | tf_op jit(solution)/shard_map/while
  719.8 6.2 collective-permute-start
  732.0 14.8 %copy-start = (bf16[512,3584]{1,0:T(8,128)(2,1)S(1)}, bf16[512,3584]{1,0:T(8,128)(2,1)}, u32[]{:S(2)}) copy-start(bf16[512,3584]{1,0:T(8,128)(2,1)} %get-tuple-element.710) | copy-start | bytes 11010052 | tf_op jit(solution)/shard_map/while
  766.3 6.2 collective-permute-start
  778.5 14.8 %copy-start = (bf16[512,3584]{1,0:T(8,128)(2,1)S(1)}, bf16[512,3584]{1,0:T(8,128)(2,1)}, u32[]{:S(2)}) copy-start(bf16[512,3584]{1,0:T(8,128)(2,1)} %get-tuple-element.710) | copy-start | bytes 11010052 | tf_op jit(solution)/shard_map/while
  812.2 6.2 collective-permute-start
  824.4 14.8 %copy-start = (bf16[512,3584]{1,0:T(8,128)(2,1)S(1)}, bf16[512,3584]{1,0:T(8,128)(2,1)}, u32[]{:S(2)}) copy-start(bf16[512,3584]{1,0:T(8,128)(2,1)} %get-tuple-element.710) | copy-start | bytes 11010052 | tf_op jit(solution)/shard_map/while
  858.7 6.2 collective-permute-start
  870.9 14.8 %copy-start = (bf16[512,3584]{1,0:T(8,128)(2,1)S(1)}, bf16[512,3584]{1,0:T(8,128)(2,1)}, u32[]{:S(2)}) copy-start(bf16[512,3584]{1,0:T(8,128)(2,1)} %get-tuple-element.710) | copy-start | bytes 11010052 | tf_op jit(solution)/shard_map/while
  904.6 6.2 collective-permute-start
  916.8 14.8 %copy-start = (bf16[512,3584]{1,0:T(8,128)(2,1)S(1)}, bf16[512,3584]{1,0:T(8,128)(2,1)}, u32[]{:S(2)}) copy-start(bf16[512,3584]{1,0:T(8,128)(2,1)} %get-tuple-element.710) | copy-start | bytes 11010052 | tf_op jit(solution)/shard_map/while
  951.1 6.2 collective-permute-start
Sparse Core Ops, SparseCore 0:
  958.1 36.7 all-reduce.1
where the time goes:
time: 1010 us; the launch traced here: 1000 us
  blocking collectives  432 us (43%)
  waiting for transfers between devices  312 us (31%)
  local copies, waits for them, and re-layouts  99.4 us (10%)
  matrix products  73.3 us (7%)
  starting transfers between devices  56.1 us (6%)
  other arithmetic  16.3 us (2%)
  between operations  13.5 us (1%)
    all_gather x1, blocking collectives, body(): prompt_rows = lax.all_gather(prompt, 'section', axis=0, tiled=True)  89 us
    psum x7, blocking collectives, layer_step(): summed = lax.psum(contract_last(hidden, down_rows), 'tensor')  78.1 us
    all_to_all x1, waiting for transfers between devices, body(): lax.all_to_all(lax.all_to_all(gate_right, 'tensor', split_axis=2, concat_...  74.6 us
    all_to_all x1, waiting for transfers between devices, body(): lax.all_to_all(lax.all_to_all(up_right, 'tensor', split_axis=2, concat_ax...  74.6 us
    dot_general x28, matrix products, contract_last(): lax.dot_general(left_side, right_side, (((1,), (1,)), ((), ())), preferre...  69.2 us
    all_to_all x1, blocking collectives, body(): lax.all_to_all(gate_left, 'section', split_axis=0, concat_axis=2, tiled=T...  53.6 us
    all_to_all x1, blocking collectives, body(): lax.all_to_all(up_left, 'section', split_axis=0, concat_axis=2, tiled=True)  50.4 us
    all_to_all x1, blocking collectives, body(): lax.all_to_all(down_left, 'tensor', split_axis=2, concat_axis=1, tiled=True)  48.1 us
  transfers between devices with their start and end apart: 14, of which 13 were waited for; matrix products, arithmetic and copies ran while one was open for 8% of the time, Pallas kernels for 0%

commit v1 on v0

--- a/solution.py
+++ b/solution.py
@@ -68,7 +68,14 @@
     down_mask = (jnp.arange(RMAX, dtype=jnp.int32) < kept_ranks[0, 2]).astype(jnp.float32)
     norm_scale = norm_gain[0]
     own_start = tensor_rank * column_block
-    prompt_rows = lax.all_gather(prompt, "section", axis=0, tiled=True)
+    ring = [prompt]
+    for hop in range(3):
+        ring.append(lax.ppermute(ring[-1], "section", [(dev, (dev + 1) % 4) for dev in range(4)]))
+    prompt_rows = jnp.roll(
+        jnp.concatenate(ring[::-1], axis=0),
+        (lax.axis_index("section") + 1) * ring[0].shape[0],
+        axis=0,
+    )
 
     def layer_step(stream):
         float_stream = stream.astype(jnp.float32)

time: 1010 us -> 1010 us (level)
  blocking collectives: 432 us -> 343 us
  waiting for transfers between devices: 312 us -> 379 us
  starting transfers between devices: 56.1 us -> 78.3 us
    all_gather x1 -> x0, blocking collectives: 89 us -> none  [body(): prompt_rows = lax.all_gather(prompt, 'section', axis=0, tiled=True)]
    ppermute x0 -> x3, waiting for transfers between devices: none -> 66.9 us  [body(): lax.ppermute(ring[-1], 'section', [(dev, (dev + 1) % 4) for dev in range(...]
    ppermute x0 -> x3, starting transfers between devices: none -> 22.1 us  [body(): lax.ppermute(ring[-1], 'section', [(dev, (dev + 1) % 4) for dev in range(...]
    unnamed x27 -> x34, local copies, waits for them, and re-layouts: 45.7 us -> 45.8 us
  transfers between devices with their start and end apart: 14 -> 17, of which waited for: 13 -> 16; matrix products, arithmetic and copies ran while one was open for 8% -> 8% of each run, Pallas kernels for 0% -> 0%
where the time goes in v1:
time: 1010 us; the launch traced here: 1000 us
  waiting for transfers between devices  379 us (38%)
  blocking collectives  343 us (34%)
  local copies, waits for them, and re-layouts  99.4 us (10%)
  starting transfers between devices  78.3 us (8%)
  matrix products  73.3 us (7%)
  other arithmetic  16.4 us (2%)
  between operations  13.6 us (1%)
    psum x7, blocking collectives, layer_step(): summed = lax.psum(contract_last(hidden, down_rows), 'tensor')  78.1 us
    all_to_all x1, waiting for transfers between devices, body(): lax.all_to_all(lax.all_to_all(up_right, 'tensor', split_axis=2, concat_ax...  74.6 us
    all_to_all x1, waiting for transfers between devices, body(): lax.all_to_all(lax.all_to_all(gate_right, 'tensor', split_axis=2, concat_...  74.6 us
    dot_general x28, matrix products, contract_last(): lax.dot_general(left_side, right_side, (((1,), (1,)), ((), ())), preferre...  69.2 us
    ppermute x3, waiting for transfers between devices, body(): lax.ppermute(ring[-1], 'section', [(dev, (dev + 1) % 4) for dev in range(...  66.9 us
    all_to_all x1, blocking collectives, body(): lax.all_to_all(gate_left, 'section', split_axis=0, concat_axis=2, tiled=T...  53.6 us
    all_to_all x1, blocking collectives, body(): lax.all_to_all(up_left, 'section', split_axis=0, concat_axis=2, tiled=True)  50.4 us
    all_to_all x1, blocking collectives, body(): lax.all_to_all(down_left, 'tensor', split_axis=2, concat_axis=1, tiled=True)  48.1 us
  transfers between devices with their start and end apart: 17, of which 16 were waited for; matrix products, arithmetic and copies ran while one was open for 8% of the time, Pallas kernels for 0%

profile of v1, /device:TPU:0, one launch (start us, length us, event | category | flops | bytes accessed | tf_op | source)
XLA Modules:
  0.0 1003.3 jit_solution(2552745919831419530)
XLA Ops:
  6.5 6.8 copy.26
  18.2 6.8 copy.30
  25.0 36.4 %all-to-all-done.1 = bf16[4,128,3584]{1,0,2:T(4,128)(2,1)} async-done(((bf16[4,128,3584]{1,0,2:T(4,128)(2,1)}), bf16[4,128,3584]{1,0,2:T(4,128)(2,1)}, u32[]{:S(2)}, u32[]{:S(2)}) %all-to-all-start.1) | async-done | bytes 3670048 | tf_op jit(solution)/shard_map/all_to_all | solution.py:39
  66.1 6.9 copy.33
  73.0 35.7 %all-to-all-done.4 = bf16[4,128,3584]{1,0,2:T(4,128)(2,1)} async-done(((bf16[4,128,3584]{1,0,2:T(4,128)(2,1)}), bf16[4,128,3584]{1,0,2:T(4,128)(2,1)}, u32[]{:S(2)}, u32[]{:S(2)}) %all-to-all-start.4) | async-done | bytes 3670048 | tf_op jit(solution)/shard_map/all_to_all | solution.py:46
  108.7 48.1 %all_to_all.144 = bf16[4,128,3584]{1,0,2:T(4,128)(2,1)} all-to-all(bf16[4,128,3584]{1,0,2:T(4,128)(2,1)} %copy.33), channel_id=1, replica_groups=mesh['groups'=2,'tensor'=4,'section'=4] {'tensor'}, dimensions={2} | all-to-all | bytes 7340032 | tf_op jit(solution)/shard_map/all_to_all | solution.py:53
  156.8 53.6 %all_to_all.145 = bf16[4,128,2048]{2,1,0:T(8,128)(2,1)} all-to-all(bf16[4,128,2048]{2,1,0:T(8,128)(2,1)S(1)} %copy-done.6), channel_id=1, replica_groups=mesh['groups'=2,'tensor'=4,'section'=4] {'section'}, dimensions={0} | all-to-all | bytes 4194304 | tf_op jit(solution)/shard_map/all_to_all | solution.py:33
  210.4 50.4 %all_to_all.146 = bf16[4,128,2048]{2,1,0:T(8,128)(2,1)} all-to-all(bf16[4,128,2048]{2,1,0:T(8,128)(2,1)S(1)} %copy-done.7), channel_id=1, replica_groups=mesh['groups'=2,'tensor'=4,'section'=4] {'section'}, dimensions={0} | all-to-all | bytes 4194304 | tf_op jit(solution)/shard_map/all_to_all | solution.py:34
  264.4 6.9 copy.27
  271.3 40.4 %all-to-all-done.8 = bf16[4,2048,128]{2,1,0:T(8,128)(2,1)S(1)} async-done(((bf16[4,2048,128]{2,1,0:T(8,128)(2,1)}), bf16[4,2048,128]{2,1,0:T(8,128)(2,1)S(1)}, u32[]{:S(2)}, u32[]{:S(2)}) %all-to-all-start.8) | async-done | bytes 2097184 | tf_op jit(solution)/shard_map/all_to_all | solution.py:35
  317.8 6.9 copy.31
  324.7 74.6 %all-to-all-done.2 = bf16[4,512,896]{2,1,0:T(8,128)(2,1)} async-done(((bf16[4,512,896]{2,1,0:T(8,128)(2,1)}), bf16[4,512,896]{2,1,0:T(8,128)(2,1)}, u32[]{:S(2)}, u32[]{:S(2)}) %all-to-all-start.2) | async-done | bytes 3670048 | tf_op jit(solution)/shard_map/all_to_all | solution.py:38
  404.1 6.9 copy.34
  411.0 74.6 %all-to-all-done.5 = bf16[4,512,896]{2,1,0:T(8,128)(2,1)} async-done(((bf16[4,512,896]{2,1,0:T(8,128)(2,1)}), bf16[4,512,896]{2,1,0:T(8,128)(2,1)}, u32[]{:S(2)}, u32[]{:S(2)}) %all-to-all-start.5) | async-done | bytes 3670048 | tf_op jit(solution)/shard_map/all_to_all | solution.py:45
  492.5 62.2 %collective-permute-done.1 = bf16[16,2048]{1,0:T(8,128)(2,1)S(1)} collective-permute-done((bf16[16,2048]{1,0:T(8,128)(2,1)S(1)}, bf16[16,2048]{1,0:T(8,128)(2,1)S(1)}, u32[]{:S(2)}, u32[]{:S(2)}) %collective-permute-start.1) | collective-permute-done | bytes 65568 | tf_op jit(solution)/shard_map/ppermute | solution.py:73
  554.7 17.3 %collective-permute-start.2 = (bf16[16,2048]{1,0:T(8,128)(2,1)S(1)}, bf16[16,2048]{1,0:T(8,128)(2,1)S(1)}, u32[]{:S(2)}, u32[]{:S(2)}) collective-permute-start(bf16[16,2048]{1,0:T(8,128)(2,1)S(1)} %collective-permute-done.1), channel_id=1, source_target_pairs={{0,1},{1,2},{2,3},{3,0},{4,5},{5,6},{6,7},{7,4},{8,9},{9,10},{10,1... | collective-permute-start | bytes 196616 | tf_op jit(solution)/shard_map/ppermute | solution.py:73
  587.7 9.7 copy.36
  599.2 5.9 copy.28
  605.1 5.9 copy.37
  611.0 5.9 copy.32
  616.9 6.0 copy.38
  623.0 5.9 copy.35
  628.9 6.0 copy.39
  634.9 322.5 %while.19 = (s32[]{:T(128)}, bf16[16,2048]{1,0:T(8,128)(2,1)S(1)}, bf16[64,2048]{1,0:T(8,128)(2,1)S(1)}, pred[]{:T(512)}, bf16[64,2048]{1,0:T(8,128)(2,1)S(1)}, ...) while((s32[]{:T(128)}, bf16[16,2048]{1,0:T(8,128)(2,1)S(1)}, ...), condition=%wide.region_3.4_spmd.clone.clone, body=%wide.region_0.3_spmd.clone.clone.sunk | while | flops 278906656 | bytes 35412760 | solution.py:117
  635.0 5.8 all_gather.39
  642.4 5.2 all_gather.41
  650.5 5.2 all_gather.40
  661.0 11.4 %psum.25 = f32[16,512]{1,0:T(8,128)S(1)} all-reduce(f32[16,512]{1,0:T(8,128)S(1)} %fusion.54), channel_id=1, replica_groups=mesh['groups'=2,'tensor'=4,'section'=4] {'tensor'}, use_global_device_ids=true, to_apply=%region_2.2 | all-reduce | flops 8192 | bytes 65536 | tf_op jit(solution)/shard_map/while/body/eval_jaxpr/psum | solution.py:93
  680.2 5.8 all_gather.39
  687.6 5.2 all_gather.41
  695.7 5.2 all_gather.40
  706.2 10.9 %psum.25 = f32[16,512]{1,0:T(8,128)S(1)} all-reduce(f32[16,512]{1,0:T(8,128)S(1)} %fusion.54), channel_id=1, replica_groups=mesh['groups'=2,'tensor'=4,'section'=4] {'tensor'}, use_global_device_ids=true, to_apply=%region_2.2 | all-reduce | flops 8192 | bytes 65536 | tf_op jit(solution)/shard_map/while/body/eval_jaxpr/psum | solution.py:93
  726.1 5.8 all_gather.39
  733.6 5.2 all_gather.41
  741.7 5.2 all_gather.40
  752.1 11.4 %psum.25 = f32[16,512]{1,0:T(8,128)S(1)} all-reduce(f32[16,512]{1,0:T(8,128)S(1)} %fusion.54), channel_id=1, replica_groups=mesh['groups'=2,'tensor'=4,'section'=4] {'tensor'}, use_global_device_ids=true, to_apply=%region_2.2 | all-reduce | flops 8192 | bytes 65536 | tf_op jit(solution)/shard_map/while/body/eval_jaxpr/psum | solution.py:93
  772.6 5.8 all_gather.39
  788.1 5.2 all_gather.40
  798.6 10.9 %psum.25 = f32[16,512]{1,0:T(8,128)S(1)} all-reduce(f32[16,512]{1,0:T(8,128)S(1)} %fusion.54), channel_id=1, replica_groups=mesh['groups'=2,'tensor'=4,'section'=4] {'tensor'}, use_global_device_ids=true, to_apply=%region_2.2 | all-reduce | flops 8192 | bytes 65536 | tf_op jit(solution)/shard_map/while/body/eval_jaxpr/psum | solution.py:93
  818.6 5.8 all_gather.39
  844.6 11.4 %psum.25 = f32[16,512]{1,0:T(8,128)S(1)} all-reduce(f32[16,512]{1,0:T(8,128)S(1)} %fusion.54), channel_id=1, replica_groups=mesh['groups'=2,'tensor'=4,'section'=4] {'tensor'}, use_global_device_ids=true, to_apply=%region_2.2 | all-reduce | flops 8192 | bytes 65536 | tf_op jit(solution)/shard_map/while/body/eval_jaxpr/psum | solution.py:93
  865.0 5.8 all_gather.39
  872.5 5.2 all_gather.41
  891.0 10.9 %psum.25 = f32[16,512]{1,0:T(8,128)S(1)} all-reduce(f32[16,512]{1,0:T(8,128)S(1)} %fusion.54), channel_id=1, replica_groups=mesh['groups'=2,'tensor'=4,'section'=4] {'tensor'}, use_global_device_ids=true, to_apply=%region_2.2 | all-reduce | flops 8192 | bytes 65536 | tf_op jit(solution)/shard_map/while/body/eval_jaxpr/psum | solution.py:93
  911.0 5.8 all_gather.39
  926.5 5.2 all_gather.40
  937.0 11.4 %psum.25 = f32[16,512]{1,0:T(8,128)S(1)} all-reduce(f32[16,512]{1,0:T(8,128)S(1)} %fusion.54), channel_id=1, replica_groups=mesh['groups'=2,'tensor'=4,'section'=4] {'tensor'}, use_global_device_ids=true, to_apply=%region_2.2 | all-reduce | flops 8192 | bytes 65536 | tf_op jit(solution)/shard_map/while/body/eval_jaxpr/psum | solution.py:93
  958.2 36.8 %all-reduce.2.cloned.1.call-done = bf16[64,2048]{1,0:T(8,128)(2,1)} async-done(((bf16[64,2048]{1,0:T(8,128)(2,1)}), bf16[64,2048]{1,0:T(8,128)(2,1)}) %all-reduce.2.cloned.1.call-update) | async-done | bytes 262160 | tf_op jit(solution)/shard_map/psum | solution.py:17
  (167 shorter events, 207.2 us)
Async XLA Ops:
  13.4 48.0 %all-to-all-start.1 = ((bf16[4,128,3584]{1,0,2:T(4,128)(2,1)}), bf16[4,128,3584]{1,0,2:T(4,128)(2,1)}, u32[]{:S(2)}, u32[]{:S(2)}) async-start(bf16[4,128,3584]{1,0,2:T(4,128)(2,1)} %copy.26), calls=%async_computation.1 | async-start | bytes 7340032 | tf_op jit(solution)/shard_map/all_to_all | solution.py:39
  61.4 47.3 %all-to-all-start.4 = ((bf16[4,128,3584]{1,0,2:T(4,128)(2,1)}), bf16[4,128,3584]{1,0,2:T(4,128)(2,1)}, u32[]{:S(2)}, u32[]{:S(2)}) async-start(bf16[4,128,3584]{1,0,2:T(4,128)(2,1)} %copy.30), calls=%async_computation.4 | async-start | bytes 7340032 | tf_op jit(solution)/shard_map/all_to_all | solution.py:46
  73.0 83.8 %copy-start.6 = (bf16[4,128,2048]{2,1,0:T(8,128)(2,1)S(1)}, bf16[4,128,2048]{2,1,0:T(8,128)(2,1)}, u32[]{:S(2)}) copy-start(bf16[4,128,2048]{2,1,0:T(8,128)(2,1)} %param.14) | copy-start | bytes 6291460
  156.8 53.6 %copy-start.7 = (bf16[4,128,2048]{2,1,0:T(8,128)(2,1)S(1)}, bf16[4,128,2048]{2,1,0:T(8,128)(2,1)}, u32[]{:S(2)}) copy-start(bf16[4,128,2048]{2,1,0:T(8,128)(2,1)} %param.15) | copy-start | bytes 6291460
  260.8 50.9 %all-to-all-start.8 = ((bf16[4,2048,128]{2,1,0:T(8,128)(2,1)}), bf16[4,2048,128]{2,1,0:T(8,128)(2,1)S(1)}, u32[]{:S(2)}, u32[]{:S(2)}) async-start(bf16[4,2048,128]{2,1,0:T(8,128)(2,1)} %param.19), calls=%async_computation.8 | async-start | bytes 4194304 | tf_op jit(solution)/shard_map/all_to_all | solution.py:35
  311.7 1.3 copy-start.1
  313.0 86.3 %all-to-all-start.2 = ((bf16[4,512,896]{2,1,0:T(8,128)(2,1)}), bf16[4,512,896]{2,1,0:T(8,128)(2,1)}, u32[]{:S(2)}, u32[]{:S(2)}) async-start(bf16[4,512,896]{2,1,0:T(8,128)(2,1)} %bitcast.83), calls=%async_computation.2 | async-start | bytes 7340032 | tf_op jit(solution)/shard_map/all_to_all | solution.py:38
  399.3 86.3 %all-to-all-start.5 = ((bf16[4,512,896]{2,1,0:T(8,128)(2,1)}), bf16[4,512,896]{2,1,0:T(8,128)(2,1)}, u32[]{:S(2)}, u32[]{:S(2)}) async-start(bf16[4,512,896]{2,1,0:T(8,128)(2,1)} %bitcast.82), calls=%async_computation.5 | async-start | bytes 7340032 | tf_op jit(solution)/shard_map/all_to_all | solution.py:45
  485.6 4.9 copy-start.8
  485.6 91.2 %copy-start.9 = (s32[1,3]{1,0:T(1,128)S(1)}, s32[1,3]{1,0:T(1,128)}, u32[]{:S(2)}) copy-start(s32[1,3]{1,0:T(1,128)} %param.13) | copy-start | bytes 40
  485.6 94.7 %copy-start.4 = (bf16[4,128,2048]{2,1,0:T(8,128)(2,1)S(1)}, bf16[4,128,2048]{2,1,0:T(8,128)(2,1)}, u32[]{:S(2)}) copy-start(bf16[4,128,2048]{2,1,0:T(8,128)(2,1)} %all_to_all.145) | copy-start | bytes 6291460
  485.6 137.4 %all-to-all-start.7 = ((bf16[4,512,896]{2,1,0:T(8,128)(2,1)}), bf16[4,512,896]{2,1,0:T(8,128)(2,1)}, u32[]{:S(2)}, u32[]{:S(2)}) async-start(bf16[4,512,896]{2,1,0:T(8,128)(2,1)} %bitcast.80), calls=%async_computation.7 | async-start | bytes 7340032 | tf_op jit(solution)/shard_map/all_to_all | solution.py:52
  490.5 504.5 %all-reduce.2.cloned.1.call-start = ((), (), s32[]{:S(2)}) async-start(), calls=%async_computation.9 | async-start | bytes 524288 | tf_op jit(solution)/shard_map/psum | solution.py:17
  490.5 64.1 %collective-permute-start.1 = (bf16[16,2048]{1,0:T(8,128)(2,1)S(1)}, bf16[16,2048]{1,0:T(8,128)(2,1)S(1)}, u32[]{:S(2)}, u32[]{:S(2)}) collective-permute-start(bf16[16,2048]{1,0:T(8,128)(2,1)S(1)} %copy-done.8), channel_id=1, source_target_pairs={{0,1},{1,2},{2,3},{3,0},{4,5},{5,6},{6,7},{7,4},{8,9},{9,10},{10,1... | collective-permute-start | bytes 196616 | tf_op jit(solution)/shard_map/ppermute | solution.py:73
  554.7 19.2 %collective-permute-start.2 = (bf16[16,2048]{1,0:T(8,128)(2,1)S(1)}, bf16[16,2048]{1,0:T(8,128)(2,1)S(1)}, u32[]{:S(2)}, u32[]{:S(2)}) collective-permute-start(bf16[16,2048]{1,0:T(8,128)(2,1)S(1)} %collective-permute-done.1), channel_id=1, source_target_pairs={{0,1},{1,2},{2,3},{3,0},{4,5},{5,6},{6,7},{7,4},{8,9},{9,10},{10,1... | collective-permute-start | bytes 196616 | tf_op jit(solution)/shard_map/ppermute | solution.py:73
  573.9 6.2 collective-permute-start.3
  580.3 3.1 copy-start.3
  583.4 4.4 copy-start.2
  628.9 6.0 copy-start.5
  641.0 14.7 %copy-start = (bf16[512,3584]{1,0:T(8,128)(2,1)S(1)}, bf16[512,3584]{1,0:T(8,128)(2,1)}, u32[]{:S(2)}) copy-start(bf16[512,3584]{1,0:T(8,128)(2,1)} %get-tuple-element.710) | copy-start | bytes 11010052 | tf_op jit(solution)/shard_map/while
  675.3 4.9 collective-permute-start
  686.2 14.7 %copy-start = (bf16[512,3584]{1,0:T(8,128)(2,1)S(1)}, bf16[512,3584]{1,0:T(8,128)(2,1)}, u32[]{:S(2)}) copy-start(bf16[512,3584]{1,0:T(8,128)(2,1)} %get-tuple-element.710) | copy-start | bytes 11010052 | tf_op jit(solution)/shard_map/while
  719.9 6.2 collective-permute-start
  732.1 14.7 %copy-start = (bf16[512,3584]{1,0:T(8,128)(2,1)S(1)}, bf16[512,3584]{1,0:T(8,128)(2,1)}, u32[]{:S(2)}) copy-start(bf16[512,3584]{1,0:T(8,128)(2,1)} %get-tuple-element.710) | copy-start | bytes 11010052 | tf_op jit(solution)/shard_map/while
  766.4 6.2 collective-permute-start
  778.6 14.7 %copy-start = (bf16[512,3584]{1,0:T(8,128)(2,1)S(1)}, bf16[512,3584]{1,0:T(8,128)(2,1)}, u32[]{:S(2)}) copy-start(bf16[512,3584]{1,0:T(8,128)(2,1)} %get-tuple-element.710) | copy-start | bytes 11010052 | tf_op jit(solution)/shard_map/while
  812.4 6.2 collective-permute-start
  824.6 14.7 %copy-start = (bf16[512,3584]{1,0:T(8,128)(2,1)S(1)}, bf16[512,3584]{1,0:T(8,128)(2,1)}, u32[]{:S(2)}) copy-start(bf16[512,3584]{1,0:T(8,128)(2,1)} %get-tuple-element.710) | copy-start | bytes 11010052 | tf_op jit(solution)/shard_map/while
  858.8 6.2 collective-permute-start
  871.0 14.7 %copy-start = (bf16[512,3584]{1,0:T(8,128)(2,1)S(1)}, bf16[512,3584]{1,0:T(8,128)(2,1)}, u32[]{:S(2)}) copy-start(bf16[512,3584]{1,0:T(8,128)(2,1)} %get-tuple-element.710) | copy-start | bytes 11010052 | tf_op jit(solution)/shard_map/while
  904.8 6.2 collective-permute-start
  917.0 14.7 %copy-start = (bf16[512,3584]{1,0:T(8,128)(2,1)S(1)}, bf16[512,3584]{1,0:T(8,128)(2,1)}, u32[]{:S(2)}) copy-start(bf16[512,3584]{1,0:T(8,128)(2,1)} %get-tuple-element.710) | copy-start | bytes 11010052 | tf_op jit(solution)/shard_map/while
  951.3 6.2 collective-permute-start
Sparse Core Ops, SparseCore 0:
  958.3 36.6 all-reduce.1
